TPU v7x, 32 devices: a whole 2x2x4 slice. The times are simulated.
32 devices in a mesh: ha: 8 (over z, core), wa: 4 (over y, x).
Axes of the slice: x: 2, y: 2, z: 4, core: 2. Of those that a mesh axis runs over, the one named last changes fastest.
Arguments:
- latents: bfloat16 [64, 64, 64, 512], P('ha', 'wa'), may hold values from -8 to 8
- cotangent: bfloat16 [64, 64, 64, 512], P('ha', 'wa'), may hold values from -0.59765625 to 0.59765625
- w_down: bfloat16 [512, 18], replicated, may hold values from -0.25 to 0.25
- bit_bias: float32 [18], replicated, may hold values from -1.5 to 1.5
- w_up: bfloat16 [18, 512], replicated, may hold values from -1.5 to 1.5
Outputs:
- grad_latents: bfloat16 [64, 64, 64, 512], P('ha', 'wa')
- bit_entropy: float32 [64, 64, 64], P('ha', 'wa')
- marginal: float32 [18], replicated
- grad_down: float32 [512, 18], replicated
- grad_bias: float32 [18], replicated
- grad_up: float32 [18, 512], replicated
All inputs are finite; a program needn't handle non-finite values.
Results may differ from a plain program's by a relative error of at most 0.005.
Values may be sent and summed in bfloat16 or wider, within the bound.
No kernel may reach another device: no remote copies, remote signals or barrier semaphores. Data moves between devices by JAX's collectives and lax.ppermute only.
A program may use at most 128 MiB of HBM per device.

v0:
```python
import jax
import jax.numpy as jnp
from jax import lax
from jax.sharding import PartitionSpec as P

local_weight = 4.0
margin_weight = 4.0


def extended_2(cells, sides, width):
    for axis, dim in sides:
        count = lax.axis_size(axis)
        head = lax.slice_in_dim(cells, 0, width, axis=dim)
        tail = lax.slice_in_dim(cells, cells.shape[dim] - width, cells.shape[dim], axis=dim)
        cells = jnp.concatenate(
            [
                lax.ppermute(tail, axis, [(i, (i + 1) % count) for i in range(count)]),
                cells,
                lax.ppermute(head, axis, [((i + 1) % count, i) for i in range(count)]),
            ],
            axis=dim,
        )
    return cells


def window(extended, rows, cols):
    total = extended[0:rows, 0:cols]
    for first in range(3):
        for second in range(3):
            if first or second:
                total = total + extended[first : first + rows, second : second + cols]
    return total / 9.0


def binary(values):
    return -values * jnp.log(values) - (1.0 - values) * jnp.log1p(-values)


def local(latents, cotangent, w_down, bit_bias, w_up):
    rows, cols, images, width = latents.shape
    bits = w_down.shape[1]
    count = rows * cols * images * lax.axis_size("ha") * lax.axis_size("wa")
    flattened = latents.reshape(-1, width)
    outward = cotangent.reshape(-1, width)
    layers = 1
    logits = jnp.dot(flattened, w_down, preferred_element_type=jnp.float32) + bit_bias
    squash = jax.nn.sigmoid(logits)
    prob = 0.01 + 0.98 * squash
    wide_prob = extended_2(prob.reshape(rows, cols, images, bits), (("ha", 0), ("wa", 1)), layers)
    local_mass = jnp.sum(prob, axis=0) / count
    marginal = lax.psum(local_mass, ("ha", "wa"))
    wide_pooled = window(wide_prob, rows + 2 * layers - 2, cols + 2 * layers - 2)
    slope = local_weight * jnp.log((1.0 - wide_pooled) / wide_pooled)
    wide_slope = extended_2(slope, (("ha", 0), ("wa", 1)), 1)
    bit_entropy = jnp.sum(binary(wide_pooled), axis=-1)
    code = (2.0 * squash - 1.0).astype(jnp.bfloat16)
    code_grad = jnp.dot(outward, w_up.T, preferred_element_type=jnp.float32)
    spread = window(wide_slope, rows, cols).reshape(-1, bits)
    steepness = squash * (1.0 - squash)
    base = ((2.0 * code_grad + 0.98 * spread) * steepness).astype(jnp.bfloat16)
    stacked = jnp.concatenate([base, steepness.astype(jnp.bfloat16)], axis=1)
    latent_part = (
        lax.dot_general(
            flattened, stacked, (((0,), (0,)), ((), ())), preferred_element_type=jnp.float32
        )
        / count
    )
    column_part = jnp.sum(stacked.astype(jnp.float32), axis=0) / count
    up_part = (
        lax.dot_general(code, outward, (((0,), (0,)), ((), ())), preferred_element_type=jnp.float32)
        / count
    )
    latent_total, column_total, grad_up = lax.psum(
        (latent_part, column_part, up_part), ("ha", "wa")
    )
    drift = margin_weight * jnp.log((1.0 - marginal) / marginal)
    logit_grad = ((2.0 * code_grad + 0.98 * (spread - drift)) * steepness).astype(jnp.bfloat16)
    grad_latents = jnp.dot(logit_grad, w_down.T, preferred_element_type=jnp.float32).astype(
        jnp.bfloat16
    )
    grad_latents = grad_latents.reshape(latents.shape)
    grad_down = latent_total[:, :bits] - 0.98 * drift * latent_total[:, bits:]
    grad_bias = column_total[:bits] - 0.98 * drift * column_total[bits:]
    return (grad_latents, bit_entropy, marginal, grad_down, grad_bias, grad_up)


def solution(mesh):
    placed = (P("ha", "wa", None, None), P("ha", "wa", None, None), P(), P(), P())
    return jax.shard_map(
        local,
        mesh=mesh,
        in_specs=placed,
        out_specs=(P("ha", "wa", None, None), P("ha", "wa", None), P(), P(), P(), P()),
        check_vma=False,
    )
```

profile of v0, /device:TPU:8, one launch (start us, length us, event | category | flops | bytes accessed | tf_op | source)
XLA Modules:
  0.0 191.5 jit_solution(5777653072572231376)
XLA Ops:
  7.2 0.0 copy-start
  7.2 0.0 all-reduce.3.cloned.1.call-start
  7.2 0.7 copy-done
  7.9 5.7 %multiply_add_fusion = (f32[8192,18]{0,1:T(8,128)S(1)}, f32[8192,18]{0,1:T(8,128)S(1)}) fusion(f32[18]{0:T(128)} %param.8, bf16[8192,512]{1,0:T(8,128)(2,1)} %bitcast.26, bf16[512,18]{0,1:T(8,128)(2,1)S(1)} %copy-done), kind=kOutput, calls=%fused_computation.59 | convolution fusion | flops 151879680 | bytes 9586760 | tf_op jit(solution)/shard_map/dot_general | solution.py:46
  13.6 0.1 slice.107
  13.7 0.0 collective-permute-start
  13.8 0.1 slice.109
  13.9 1.8 collective-permute-start.1
  15.6 0.5 reshape.34
  16.1 2.2 %collective-permute-done = f32[1,16,64,18]{2,1,0,3:T(8,128)S(1)} collective-permute-done((f32[1,16,64,18]{2,1,0,3:T(8,128)S(1)}, f32[1,16,64,18]{2,1,0,3:T(8,128)S(1)}, u32[]{:S(2)}, u32[]{:S(2)}) %collective-permute-start) | collective-permute-done | bytes 73760 | tf_op jit(solution)/shard_map/ppermute | solution.py:17
  18.3 0.1 constant_dynamic-update-slice_fusion.1
  18.4 0.7 collective-permute-done.1
  19.2 0.1 fusion.42
  19.3 2.0 %collective-permute-start.2 = (f32[10,1,64,18]{2,1,0,3:T(1,128)S(1)}, f32[10,1,64,18]{2,1,0,3:T(1,128)S(1)}, u32[]{:S(2)}, u32[]{:S(2)}) collective-permute-start(f32[10,1,64,18]{2,1,0,3:T(1,128)S(1)} %get-tuple-element.17), channel_id=1, source_target_pairs={{0,1},{1,2},{2,3},{3,0},{4,5},{5,6},{6,7},{7,4},{8,9},{9,10},{10,1... | collective-permute-start | bytes 138248 | tf_op jit(solution)/shard_map/ppermute | solution.py:17
  21.4 1.0 collective-permute-start.3
  22.4 3.3 %collective-permute-done.2 = f32[10,1,64,18]{2,1,0,3:T(1,128)S(1)} collective-permute-done((f32[10,1,64,18]{2,1,0,3:T(1,128)S(1)}, f32[10,1,64,18]{2,1,0,3:T(1,128)S(1)}, u32[]{:S(2)}, u32[]{:S(2)}) %collective-permute-start.2) | collective-permute-done | bytes 46112 | tf_op jit(solution)/shard_map/ppermute | solution.py:17
  25.7 2.5 %collective-permute-done.3 = f32[10,1,64,18]{2,1,0,3:T(1,128)S(1)} collective-permute-done((f32[10,1,64,18]{2,1,0,3:T(1,128)S(1)}, f32[10,1,64,18]{2,1,0,3:T(1,128)S(1)}, u32[]{:S(2)}, u32[]{:S(2)}) %collective-permute-start.3) | collective-permute-done | bytes 46112 | tf_op jit(solution)/shard_map/ppermute | solution.py:19
  28.2 3.1 %fusion.7 = (f32[8,16,64]{2,1,0:T(8,128)}, f32[8,16,64,18]{2,1,0,3:T(8,128)S(1)}) fusion(f32[10,1,64,18]{2,1,0,3:T(1,128)S(1)} %collective-permute-done.3, f32[10,16,64,18]{2,1,0,3:T(8,128)S(1)} %constant_dynamic-update-slice_fusion, f32[1,16,64,18]{2,1,0,3:T(8,128)S(1)} %collective-permute-done.1, f32[8,16,64,18]{2,1,0,3:T(8,128)S(1)} %reshape.34, ...), kind=kLoop, calls=%fused_computation.24 | loop fusion | flops 3383296 | bytes 2189312 | tf_op jit(solution)/shard_map/reduce_sum | solution.py:55
  31.4 0.3 fusion.5
  31.7 0.1 collective-permute-start.4
  31.8 1.7 collective-permute-start.5
  33.5 2.8 %collective-permute-done.4 = f32[1,16,64,18]{2,1,0,3:T(8,128)S(1)} collective-permute-done((f32[1,16,64,18]{2,1,0,3:T(8,128)S(1)}, f32[1,16,64,18]{2,1,0,3:T(8,128)S(1)}, u32[]{:S(2)}, u32[]{:S(2)}) %collective-permute-start.4) | collective-permute-done | bytes 73760 | tf_op jit(solution)/shard_map/ppermute | solution.py:17
  36.3 0.7 collective-permute-done.5
  37.0 0.2 pad_maximum_fusion.11
  37.2 1.6 collective-permute-start.6
  38.8 1.4 collective-permute-start.7
  40.2 4.6 %convolution_multiply_fusion.2 = f32[18,512]{1,0:T(8,128)S(1)} fusion(bf16[8192,512]{1,0:T(8,128)(2,1)} %bitcast.24, f32[8192,18]{0,1:T(8,128)S(1)} %get-tuple-element.29), kind=kOutput, calls=%fused_computation.55 | convolution fusion | flops 151446528 | bytes 9015296 | tf_op jit(solution)/shard_map/dot_general | solution.py:70
  44.7 0.0 collective-permute-done.6
  44.8 0.0 collective-permute-done.7
  44.8 0.4 maximum_maximum_fusion
  45.2 0.7 fusion.21
  45.9 0.0 copy-start.1
  45.9 0.4 reshape.35
  46.3 0.3 copy-done.1
  46.7 5.8 %multiply_convert_fusion = (bf16[8192,18]{0,1:T(8,128)(2,1)S(1)}, f32[18]{0:T(128)S(1)}, bf16[8192,18]{0,1:T(8,128)(2,1)S(1)}, f32[8192,18]{0,1:T(8,128)S(1)}) fusion(f32[8192,18]{0,1:T(8,128)S(1)} %reshape.35, f32[8192,18]{0,1:T(8,128)S(1)} %get-tuple-element.29, bf16[8192,512]{1,0:T(8,128)(2,1)} %bitcast.25, bf16[18,512]{1,0:T(8,128)(2,1)S(1)} %copy-done.1), kind=kOutput, calls=%fused_computation.57 | convolution fusion | flops 152616944 | bytes 10766408 | tf_op jit(solution)/shard_map/dot_general | solution.py:57
  52.5 0.3 convert_reduce_fusion
  52.7 5.3 %fusion.25 = f32[512,36]{0,1:T(8,128)} fusion(bf16[8192,512]{1,0:T(8,128)(2,1)} %bitcast.27, bf16[8192,18]{0,1:T(8,128)(2,1)S(1)} %get-tuple-element.23, bf16[8192,18]{0,1:T(8,128)(2,1)S(1)} %get-tuple-element.21), kind=kOutput, calls=%fused_computation.54 | convolution fusion | flops 303187968 | bytes 9052160 | tf_op jit(solution)/shard_map/dot_general | solution.py:63
  58.0 0.0 all-reduce.3.cloned.1.call-update
  58.1 42.2 %all-reduce = (f32[18]{0:T(128)S(1)}, f32[36]{0:T(128)S(1)}, f32[18,512]{1,0:T(8,128)}) all-reduce(f32[18]{0:T(128)S(1)} %broadcast_multiply_fusion.3, f32[36]{0:T(128)S(1)} %broadcast_multiply_fusion, f32[18,512]{1,0:T(8,128)S(1)} %convolution_multiply_fusion.2), channel_id=1, replica_groups=mesh['ha'=8,'wa'=4] {'ha','wa'}, use_global_device_ids=true, to_apply=%region_1.0 | all-reduce | flops 9270 | bytes 74160 | tf_op jit(solution)/shard_map/psum | solution.py:51
  100.2 0.0 copy-start.2
  100.2 0.6 multiply_subtract_fusion
  100.8 5.9 %convolution_convert_fusion = bf16[8192,512]{1,0:T(8,128)(2,1)} fusion(bf16[512,18]{0,1:T(8,128)(2,1)S(1)} %copy-done, f32[8192,18]{0,1:T(8,128)S(1)} %get-tuple-element.30, f32[8192,18]{0,1:T(8,128)S(1)} %reshape.35, f32[8192,18]{0,1:T(8,128)S(1)} %get-tuple-element.29, f32[18]{0:T(128)S(1)} %get-tuple-element.27), kind=kOutput, calls=%fused_computation | convolution fusion | flops 156221440 | bytes 10176584 | tf_op jit(solution)/shard_map/dot_general | solution.py:78
  106.7 0.0 copy-done.2
  106.7 76.4 %all-reduce.3.cloned.1.call-done = f32[512,36]{0,1:T(8,128)} async-done(((f32[512,36]{0,1:T(8,128)}), f32[512,36]{0,1:T(8,128)}) %all-reduce.3.cloned.1.call-update) | async-done | bytes 73744 | tf_op jit(solution)/shard_map/psum | solution.py:73
  183.1 1.6 fusion.32
  (7 shorter events, 0.1 us)
Async XLA Ops:
  7.2 0.7 copy-start
  7.2 176.0 %all-reduce.3.cloned.1.call-start = ((), (), s32[]{:S(2)}) async-start(), calls=%async_computation | async-start | bytes 163840 | tf_op jit(solution)/shard_map/psum | solution.py:73
  13.7 4.6 %collective-permute-start = (f32[1,16,64,18]{2,1,0,3:T(8,128)S(1)}, f32[1,16,64,18]{2,1,0,3:T(8,128)S(1)}, u32[]{:S(2)}, u32[]{:S(2)}) collective-permute-start(f32[1,16,64,18]{2,1,0,3:T(8,128)S(1)} %bitcast.29), channel_id=1, source_target_pairs={{0,4},{4,8},{8,12},{12,16},{16,20},{20,24},{24,28},{28,0},{1,5},{5... | collective-permute-start | bytes 221192 | tf_op jit(solution)/shard_map/ppermute | solution.py:17
  13.9 5.3 %collective-permute-start.1 = (f32[1,16,64,18]{2,1,0,3:T(8,128)S(1)}, f32[1,16,64,18]{2,1,0,3:T(8,128)S(1)}, u32[]{:S(2)}, u32[]{:S(2)}) collective-permute-start(f32[1,16,64,18]{2,1,0,3:T(8,128)S(1)} %bitcast.30), channel_id=1, source_target_pairs={{4,0},{8,4},{12,8},{16,12},{20,16},{24,20},{28,24},{0,28},{5,1},{9... | collective-permute-start | bytes 221192 | tf_op jit(solution)/shard_map/ppermute | solution.py:19
  19.3 6.4 %collective-permute-start.2 = (f32[10,1,64,18]{2,1,0,3:T(1,128)S(1)}, f32[10,1,64,18]{2,1,0,3:T(1,128)S(1)}, u32[]{:S(2)}, u32[]{:S(2)}) collective-permute-start(f32[10,1,64,18]{2,1,0,3:T(1,128)S(1)} %get-tuple-element.17), channel_id=1, source_target_pairs={{0,1},{1,2},{2,3},{3,0},{4,5},{5,6},{6,7},{7,4},{8,9},{9,10},{10,1... | collective-permute-start | bytes 138248 | tf_op jit(solution)/shard_map/ppermute | solution.py:17
  21.4 6.8 %collective-permute-start.3 = (f32[10,1,64,18]{2,1,0,3:T(1,128)S(1)}, f32[10,1,64,18]{2,1,0,3:T(1,128)S(1)}, u32[]{:S(2)}, u32[]{:S(2)}) collective-permute-start(f32[10,1,64,18]{2,1,0,3:T(1,128)S(1)} %get-tuple-element.18), channel_id=1, source_target_pairs={{1,0},{2,1},{3,2},{0,3},{5,4},{6,5},{7,6},{4,7},{9,8},{10,9},{11,1... | collective-permute-start | bytes 138248 | tf_op jit(solution)/shard_map/ppermute | solution.py:19
  31.7 4.6 %collective-permute-start.4 = (f32[1,16,64,18]{2,1,0,3:T(8,128)S(1)}, f32[1,16,64,18]{2,1,0,3:T(8,128)S(1)}, u32[]{:S(2)}, u32[]{:S(2)}) collective-permute-start(f32[1,16,64,18]{2,1,0,3:T(8,128)S(1)} %get-tuple-element.19), channel_id=1, source_target_pairs={{0,4},{4,8},{8,12},{12,16},{16,20},{20,24},{24,28},{28,0},{1,5},{5... | collective-permute-start | bytes 221192 | tf_op jit(solution)/shard_map/ppermute | solution.py:17
  31.8 5.3 %collective-permute-start.5 = (f32[1,16,64,18]{2,1,0,3:T(8,128)S(1)}, f32[1,16,64,18]{2,1,0,3:T(8,128)S(1)}, u32[]{:S(2)}, u32[]{:S(2)}) collective-permute-start(f32[1,16,64,18]{2,1,0,3:T(8,128)S(1)} %get-tuple-element.20), channel_id=1, source_target_pairs={{4,0},{8,4},{12,8},{16,12},{20,16},{24,20},{28,24},{0,28},{5,1},{9... | collective-permute-start | bytes 221192 | tf_op jit(solution)/shard_map/ppermute | solution.py:19
  37.2 7.6 %collective-permute-start.6 = (f32[10,1,64,18]{2,1,0,3:T(1,128)S(1)}, f32[10,1,64,18]{2,1,0,3:T(1,128)S(1)}, u32[]{:S(2)}, u32[]{:S(2)}) collective-permute-start(f32[10,1,64,18]{2,1,0,3:T(1,128)S(1)} %get-tuple-element.15), channel_id=1, source_target_pairs={{0,1},{1,2},{2,3},{3,0},{4,5},{5,6},{6,7},{7,4},{8,9},{9,10},{10,1... | collective-permute-start | bytes 138248 | tf_op jit(solution)/shard_map/ppermute | solution.py:17
  38.8 6.0 %collective-permute-start.7 = (f32[10,1,64,18]{2,1,0,3:T(1,128)S(1)}, f32[10,1,64,18]{2,1,0,3:T(1,128)S(1)}, u32[]{:S(2)}, u32[]{:S(2)}) collective-permute-start(f32[10,1,64,18]{2,1,0,3:T(1,128)S(1)} %get-tuple-element.16), channel_id=1, source_target_pairs={{1,0},{2,1},{3,2},{0,3},{5,4},{6,5},{7,6},{4,7},{9,8},{10,9},{11,1... | collective-permute-start | bytes 138248 | tf_op jit(solution)/shard_map/ppermute | solution.py:19
  45.9 0.7 copy-start.1
  100.2 6.5 %copy-start.2 = (f32[18]{0:T(128)}, f32[18]{0:T(128)S(1)}, u32[]{:S(2)}) copy-start(f32[18]{0:T(128)S(1)} %get-tuple-element.6) | copy-start | bytes 220
Sparse Core Ops, SparseCore 0:
  58.2 124.8 all-reduce.2
where the time goes:
time: 192 us
  waiting for transfers between devices  88.8 us (46%)
  blocking collectives  42.2 us (22%)
  matrix products  27.2 us (14%)
  between operations  14.2 us (7%)
  starting transfers between devices  9.68 us (5%)
  other arithmetic  7.18 us (4%)
  local copies, waits for them, and re-layouts  2.33 us (1%)
    psum x1, waiting for transfers between devices, local(): lax.psum((latent_part, column_part, up_part), ('ha', 'wa'))  76.4 us
    psum x1, blocking collectives, local(): marginal = lax.psum(local_mass, ('ha', 'wa'))  42.2 us
    ppermute x4, waiting for transfers between devices, extended_2(): lax.ppermute(tail, axis, [(i, (i + 1) % count) for i in range(count)])  8.36 us
    ppermute x4, starting transfers between devices, extended_2(): lax.ppermute(head, axis, [((i + 1) % count, i) for i in range(count)])  5.91 us
    dot_general x1, matrix products, local(): jnp.dot(logit_grad, w_down.T, preferred_element_type=jnp.float32)  5.89 us
    dot_general x1, matrix products, local(): code_grad = jnp.dot(outward, w_up.T, preferred_element_type=jnp.float32)  5.8 us
    dot_general x1, matrix products, local(): jnp.dot(flattened, w_down, preferred_element_type=jnp.float32) + bit_bias  5.7 us
    dot_general x1, matrix products, local(): lax.dot_general(flattened, stacked, (((0,), (0,)), ((), ())), preferred_e...  5.3 us
  transfers between devices with their start and end apart: 9, of which 7 were waited for; matrix products, arithmetic and copies ran while one was open for 6% of the time, Pallas kernels for 0%

commit v1 on v0

--- a/solution.py
+++ b/solution.py
@@ -48,7 +48,9 @@
     prob = 0.01 + 0.98 * squash
     wide_prob = extended_2(prob.reshape(rows, cols, images, bits), (("ha", 0), ("wa", 1)), layers)
     local_mass = jnp.sum(prob, axis=0) / count
-    marginal = lax.psum(local_mass, ("ha", "wa"))
+    marginal = local_mass
+    for nth in ("ha", "wa"):
+        marginal = lax.psum(marginal, nth)
     wide_pooled = window(wide_prob, rows + 2 * layers - 2, cols + 2 * layers - 2)
     slope = local_weight * jnp.log((1.0 - wide_pooled) / wide_pooled)
     wide_slope = extended_2(slope, (("ha", 0), ("wa", 1)), 1)

time: 192 us -> 206 us (1.073)
  blocking collectives: 42.2 us -> 65.6 us
  waiting for transfers between devices: 88.8 us -> 79.4 us
    psum x1 -> x3, blocking collectives: 42.2 us -> 65.6 us  [the longest x1 42.9 us: local(): lax.psum((latent_part, column_part, up_part), ('ha', 'wa'))]
    psum x1, waiting for transfers between devices: 76.4 us -> 67.1 us  [local(): lax.psum((latent_part, column_part, up_part), ('ha', 'wa'))]
where the time goes in v1:
time: 206 us
  waiting for transfers between devices  79.4 us (39%)
  blocking collectives  65.6 us (32%)
  matrix products  27.3 us (13%)
  between operations  14.2 us (7%)
  starting transfers between devices  9.68 us (5%)
  other arithmetic  7.18 us (3%)
  local copies, waits for them, and re-layouts  2.33 us (1%)
    psum x1, waiting for transfers between devices, local(): lax.psum((latent_part, column_part, up_part), ('ha', 'wa'))  67.1 us
    psum x1, blocking collectives, local(): lax.psum((latent_part, column_part, up_part), ('ha', 'wa'))  42.9 us
    psum x2, blocking collectives, local(): marginal = lax.psum(marginal, nth)  22.7 us
    ppermute x4, waiting for transfers between devices, extended_2(): lax.ppermute(tail, axis, [(i, (i + 1) % count) for i in range(count)])  8.36 us
    ppermute x4, starting transfers between devices, extended_2(): lax.ppermute(head, axis, [((i + 1) % count, i) for i in range(count)])  5.91 us
    dot_general x1, matrix products, local(): jnp.dot(logit_grad, w_down.T, preferred_element_type=jnp.float32)  5.89 us
    dot_general x1, matrix products, local(): code_grad = jnp.dot(outward, w_up.T, preferred_element_type=jnp.float32)  5.8 us
    dot_general x1, matrix products, local(): jnp.dot(flattened, w_down, preferred_element_type=jnp.float32) + bit_bias  5.7 us
  transfers between devices with their start and end apart: 9, of which 7 were waited for; matrix products, arithmetic and copies ran while one was open for 6% of the time, Pallas kernels for 0%

profile of v1, /device:TPU:8, one launch (start us, length us, event | category | flops | bytes accessed | tf_op | source)
XLA Modules:
  0.0 205.7 jit_solution(18036042748925786709)
XLA Ops:
  7.2 0.0 copy-start
  7.2 0.0 all-reduce.3.cloned.1.call-start
  7.2 0.7 copy-done
  7.9 5.7 %multiply_add_fusion = (f32[8192,18]{0,1:T(8,128)S(1)}, f32[8192,18]{0,1:T(8,128)S(1)}) fusion(f32[18]{0:T(128)} %param.8, bf16[8192,512]{1,0:T(8,128)(2,1)} %bitcast.26, bf16[512,18]{0,1:T(8,128)(2,1)S(1)} %copy-done), kind=kOutput, calls=%fused_computation.59 | convolution fusion | flops 151879680 | bytes 9586760 | tf_op jit(solution)/shard_map/dot_general | solution.py:46
  13.6 0.1 slice.107
  13.7 0.0 collective-permute-start
  13.8 0.1 slice.109
  13.9 1.8 collective-permute-start.1
  15.6 0.5 reshape.34
  16.1 2.2 %collective-permute-done = f32[1,16,64,18]{2,1,0,3:T(8,128)S(1)} collective-permute-done((f32[1,16,64,18]{2,1,0,3:T(8,128)S(1)}, f32[1,16,64,18]{2,1,0,3:T(8,128)S(1)}, u32[]{:S(2)}, u32[]{:S(2)}) %collective-permute-start) | collective-permute-done | bytes 73760 | tf_op jit(solution)/shard_map/ppermute | solution.py:17
  18.3 0.1 constant_dynamic-update-slice_fusion.1
  18.4 0.7 collective-permute-done.1
  19.2 0.1 fusion.42
  19.3 2.0 collective-permute-start.2
  21.4 1.0 collective-permute-start.3
  22.4 3.3 %collective-permute-done.2 = f32[10,1,64,18]{2,1,0,3:T(1,128)S(1)} collective-permute-done((f32[10,1,64,18]{2,1,0,3:T(1,128)S(1)}, f32[10,1,64,18]{2,1,0,3:T(1,128)S(1)}, u32[]{:S(2)}, u32[]{:S(2)}) %collective-permute-start.2) | collective-permute-done | bytes 46112 | tf_op jit(solution)/shard_map/ppermute | solution.py:17
  25.7 2.5 %collective-permute-done.3 = f32[10,1,64,18]{2,1,0,3:T(1,128)S(1)} collective-permute-done((f32[10,1,64,18]{2,1,0,3:T(1,128)S(1)}, f32[10,1,64,18]{2,1,0,3:T(1,128)S(1)}, u32[]{:S(2)}, u32[]{:S(2)}) %collective-permute-start.3) | collective-permute-done | bytes 46112 | tf_op jit(solution)/shard_map/ppermute | solution.py:19
  28.2 3.1 %fusion.7 = (f32[8,16,64]{2,1,0:T(8,128)}, f32[8,16,64,18]{2,1,0,3:T(8,128)S(1)}) fusion(f32[10,1,64,18]{2,1,0,3:T(1,128)S(1)} %collective-permute-done.3, f32[10,16,64,18]{2,1,0,3:T(8,128)S(1)} %constant_dynamic-update-slice_fusion, f32[1,16,64,18]{2,1,0,3:T(8,128)S(1)} %collective-permute-done.1, f32[8,16,64,18]{2,1,0,3:T(8,128)S(1)} %reshape.34, ...), kind=kLoop, calls=%fused_computation.24 | loop fusion | flops 3383296 | bytes 2189312 | tf_op jit(solution)/shard_map/reduce_sum | solution.py:57
  31.4 0.3 fusion.5
  31.7 0.1 collective-permute-start.4
  31.8 1.7 collective-permute-start.5
  33.5 2.8 %collective-permute-done.4 = f32[1,16,64,18]{2,1,0,3:T(8,128)S(1)} collective-permute-done((f32[1,16,64,18]{2,1,0,3:T(8,128)S(1)}, f32[1,16,64,18]{2,1,0,3:T(8,128)S(1)}, u32[]{:S(2)}, u32[]{:S(2)}) %collective-permute-start.4) | collective-permute-done | bytes 73760 | tf_op jit(solution)/shard_map/ppermute | solution.py:17
  36.3 0.7 collective-permute-done.5
  37.0 0.2 pad_maximum_fusion.11
  37.2 1.6 collective-permute-start.6
  38.8 1.4 collective-permute-start.7
  40.2 4.6 %convolution_multiply_fusion.2 = f32[18,512]{1,0:T(8,128)S(1)} fusion(bf16[8192,512]{1,0:T(8,128)(2,1)} %bitcast.24, f32[8192,18]{0,1:T(8,128)S(1)} %get-tuple-element.28), kind=kOutput, calls=%fused_computation.55 | convolution fusion | flops 151446528 | bytes 9015296 | tf_op jit(solution)/shard_map/dot_general | solution.py:72
  44.7 0.0 collective-permute-done.6
  44.8 0.0 collective-permute-done.7
  44.8 0.4 maximum_maximum_fusion
  45.2 0.7 fusion.21
  45.9 0.0 copy-start.1
  45.9 0.4 reshape.35
  46.3 0.3 copy-done.1
  46.7 5.8 %fusion.39 = (f32[18]{0:T(128)S(1)}, bf16[8192,18]{0,1:T(8,128)(2,1)S(1)}, bf16[8192,18]{0,1:T(8,128)(2,1)S(1)}, f32[8192,18]{0,1:T(8,128)S(1)}) fusion(f32[8192,18]{0,1:T(8,128)S(1)} %get-tuple-element.28, f32[8192,18]{0,1:T(8,128)S(1)} %reshape.35, bf16[8192,512]{1,0:T(8,128)(2,1)} %bitcast.25, bf16[18,512]{1,0:T(8,128)(2,1)S(1)} %copy-done.1), kind=kOutput, calls=%fused_computation.87 | convolution fusion | flops 152616944 | bytes 10766408 | tf_op jit(solution)/shard_map/dot_general | solution.py:59
  52.5 0.3 convert_reduce_fusion
  52.7 5.3 %fusion.25 = f32[512,36]{0,1:T(8,128)} fusion(bf16[8192,512]{1,0:T(8,128)(2,1)} %bitcast.27, bf16[8192,18]{0,1:T(8,128)(2,1)S(1)} %get-tuple-element.22, bf16[8192,18]{0,1:T(8,128)(2,1)S(1)} %get-tuple-element.21), kind=kOutput, calls=%fused_computation.54 | convolution fusion | flops 303187968 | bytes 9052160 | tf_op jit(solution)/shard_map/dot_general | solution.py:65
  58.0 14.6 %psum.35 = f32[18]{0:T(128)S(1)} all-reduce(f32[18]{0:T(128)S(1)} %broadcast_multiply_fusion.3), channel_id=1, replica_groups=mesh['ha'=8,'wa'=4] {'ha'}, use_global_device_ids=true, to_apply=%region_1.0 | all-reduce | flops 18 | bytes 144 | tf_op jit(solution)/shard_map/psum | solution.py:53
  72.7 0.0 all-reduce.3.cloned.1.call-update
  72.7 8.1 %psum.36 = f32[18]{0:T(128)S(1)} all-reduce(f32[18]{0:T(128)S(1)} %psum.35), channel_id=1, replica_groups=mesh['ha'=8,'wa'=4] {'wa'}, use_global_device_ids=true, to_apply=%region_2.0 | all-reduce | flops 18 | bytes 144 | tf_op jit(solution)/shard_map/psum | solution.py:53
  80.8 0.0 copy-start.2
  80.8 42.9 %all-reduce = (f32[36]{0:T(128)S(1)}, f32[18,512]{1,0:T(8,128)}) all-reduce(f32[36]{0:T(128)S(1)} %broadcast_multiply_fusion, f32[18,512]{1,0:T(8,128)S(1)} %convolution_multiply_fusion.2), channel_id=1, replica_groups=mesh['ha'=8,'wa'=4] {'ha','wa'}, use_global_device_ids=true, to_apply=%region_6.0 | all-reduce | flops 9252 | bytes 74016 | tf_op jit(solution)/shard_map/psum | solution.py:75
  123.7 0.6 multiply_subtract_fusion
  124.3 5.9 %convolution_convert_fusion = bf16[8192,512]{1,0:T(8,128)(2,1)} fusion(bf16[512,18]{0,1:T(8,128)(2,1)S(1)} %copy-done, f32[8192,18]{0,1:T(8,128)S(1)} %get-tuple-element.29, f32[8192,18]{0,1:T(8,128)S(1)} %reshape.35, f32[8192,18]{0,1:T(8,128)S(1)} %get-tuple-element.28, f32[18]{0:T(128)S(1)} %get-tuple-element.26), kind=kOutput, calls=%fused_computation | convolution fusion | flops 156221440 | bytes 10176584 | tf_op jit(solution)/shard_map/dot_general | solution.py:80
  130.2 0.0 copy-done.2
  130.2 67.1 %all-reduce.3.cloned.1.call-done = f32[512,36]{0,1:T(8,128)} async-done(((f32[512,36]{0,1:T(8,128)}), f32[512,36]{0,1:T(8,128)}) %all-reduce.3.cloned.1.call-update) | async-done | bytes 73744 | tf_op jit(solution)/shard_map/psum | solution.py:75
  197.2 1.6 fusion.32
  (7 shorter events, 0.1 us)
Async XLA Ops:
  7.2 0.7 copy-start
  7.2 190.1 %all-reduce.3.cloned.1.call-start = ((), (), s32[]{:S(2)}) async-start(), calls=%async_computation | async-start | bytes 163840 | tf_op jit(solution)/shard_map/psum | solution.py:75
  13.7 4.6 %collective-permute-start = (f32[1,16,64,18]{2,1,0,3:T(8,128)S(1)}, f32[1,16,64,18]{2,1,0,3:T(8,128)S(1)}, u32[]{:S(2)}, u32[]{:S(2)}) collective-permute-start(f32[1,16,64,18]{2,1,0,3:T(8,128)S(1)} %bitcast.29), channel_id=1, source_target_pairs={{0,4},{4,8},{8,12},{12,16},{16,20},{20,24},{24,28},{28,0},{1,5},{5... | collective-permute-start | bytes 221192 | tf_op jit(solution)/shard_map/ppermute | solution.py:17
  13.9 5.3 %collective-permute-start.1 = (f32[1,16,64,18]{2,1,0,3:T(8,128)S(1)}, f32[1,16,64,18]{2,1,0,3:T(8,128)S(1)}, u32[]{:S(2)}, u32[]{:S(2)}) collective-permute-start(f32[1,16,64,18]{2,1,0,3:T(8,128)S(1)} %bitcast.30), channel_id=1, source_target_pairs={{4,0},{8,4},{12,8},{16,12},{20,16},{24,20},{28,24},{0,28},{5,1},{9... | collective-permute-start | bytes 221192 | tf_op jit(solution)/shard_map/ppermute | solution.py:19
  19.3 6.4 %collective-permute-start.2 = (f32[10,1,64,18]{2,1,0,3:T(1,128)S(1)}, f32[10,1,64,18]{2,1,0,3:T(1,128)S(1)}, u32[]{:S(2)}, u32[]{:S(2)}) collective-permute-start(f32[10,1,64,18]{2,1,0,3:T(1,128)S(1)} %get-tuple-element.16), channel_id=1, source_target_pairs={{0,1},{1,2},{2,3},{3,0},{4,5},{5,6},{6,7},{7,4},{8,9},{9,10},{10,1... | collective-permute-start | bytes 138248 | tf_op jit(solution)/shard_map/ppermute | solution.py:17
  21.4 6.8 %collective-permute-start.3 = (f32[10,1,64,18]{2,1,0,3:T(1,128)S(1)}, f32[10,1,64,18]{2,1,0,3:T(1,128)S(1)}, u32[]{:S(2)}, u32[]{:S(2)}) collective-permute-start(f32[10,1,64,18]{2,1,0,3:T(1,128)S(1)} %get-tuple-element.17), channel_id=1, source_target_pairs={{1,0},{2,1},{3,2},{0,3},{5,4},{6,5},{7,6},{4,7},{9,8},{10,9},{11,1... | collective-permute-start | bytes 138248 | tf_op jit(solution)/shard_map/ppermute | solution.py:19
  31.7 4.6 %collective-permute-start.4 = (f32[1,16,64,18]{2,1,0,3:T(8,128)S(1)}, f32[1,16,64,18]{2,1,0,3:T(8,128)S(1)}, u32[]{:S(2)}, u32[]{:S(2)}) collective-permute-start(f32[1,16,64,18]{2,1,0,3:T(8,128)S(1)} %get-tuple-element.18), channel_id=1, source_target_pairs={{0,4},{4,8},{8,12},{12,16},{16,20},{20,24},{24,28},{28,0},{1,5},{5... | collective-permute-start | bytes 221192 | tf_op jit(solution)/shard_map/ppermute | solution.py:17
  31.8 5.3 %collective-permute-start.5 = (f32[1,16,64,18]{2,1,0,3:T(8,128)S(1)}, f32[1,16,64,18]{2,1,0,3:T(8,128)S(1)}, u32[]{:S(2)}, u32[]{:S(2)}) collective-permute-start(f32[1,16,64,18]{2,1,0,3:T(8,128)S(1)} %get-tuple-element.19), channel_id=1, source_target_pairs={{4,0},{8,4},{12,8},{16,12},{20,16},{24,20},{28,24},{0,28},{5,1},{9... | collective-permute-start | bytes 221192 | tf_op jit(solution)/shard_map/ppermute | solution.py:19
  37.2 7.6 %collective-permute-start.6 = (f32[10,1,64,18]{2,1,0,3:T(1,128)S(1)}, f32[10,1,64,18]{2,1,0,3:T(1,128)S(1)}, u32[]{:S(2)}, u32[]{:S(2)}) collective-permute-start(f32[10,1,64,18]{2,1,0,3:T(1,128)S(1)} %get-tuple-element.14), channel_id=1, source_target_pairs={{0,1},{1,2},{2,3},{3,0},{4,5},{5,6},{6,7},{7,4},{8,9},{9,10},{10,1... | collective-permute-start | bytes 138248 | tf_op jit(solution)/shard_map/ppermute | solution.py:17
  38.8 6.0 %collective-permute-start.7 = (f32[10,1,64,18]{2,1,0,3:T(1,128)S(1)}, f32[10,1,64,18]{2,1,0,3:T(1,128)S(1)}, u32[]{:S(2)}, u32[]{:S(2)}) collective-permute-start(f32[10,1,64,18]{2,1,0,3:T(1,128)S(1)} %get-tuple-element.15), channel_id=1, source_target_pairs={{1,0},{2,1},{3,2},{0,3},{5,4},{6,5},{7,6},{4,7},{9,8},{10,9},{11,1... | collective-permute-start | bytes 138248 | tf_op jit(solution)/shard_map/ppermute | solution.py:19
  45.9 0.7 copy-start.1
  80.8 49.4 %copy-start.2 = (f32[18]{0:T(128)}, f32[18]{0:T(128)S(1)}, u32[]{:S(2)}) copy-start(f32[18]{0:T(128)S(1)} %psum.36) | copy-start | bytes 220
Sparse Core Ops, SparseCore 0:
  72.8 124.3 all-reduce.2
